TPU v7x, 32 devices: a whole 2x2x4 slice. The times are simulated.
32 devices in a mesh: dp: 4 (over x, core), tensor: 8 (over z, y).
Axes of the slice: x: 2, y: 2, z: 4, core: 2. Of those that a mesh axis runs over, the one named last changes fastest.
Arguments:
- hidden_in: bfloat16 [8192, 2048], P('dp'), may hold values from -6 to 6
- seq_lengths: int32 [4], P('dp'), may hold values from 1024 to 2048, as said below
- out_grad: bfloat16 [8192, 2048], P('dp'), may hold values from -6 to 6
- attn_gain: float32 [2048], replicated, may hold values from 0.5 to 1.5
- mlp_gain: float32 [2048], replicated, may hold values from 0.5 to 1.5
- w_query: bfloat16 [2048, 2048], P(None, 'tensor'), may hold values from -0.5 to 0.5
- w_key: bfloat16 [2048, 512], P('tensor'), may hold values from -0.5 to 0.5
- w_value: bfloat16 [2048, 512], P('tensor'), may hold values from -0.125 to 0.125
- w_out: bfloat16 [2048, 2048], P('tensor'), may hold values from -2 to 2
- w_gate: bfloat16 [2048, 8192], P(None, 'tensor'), may hold values from -0.125 to 0.125
- w_up: bfloat16 [2048, 8192], P(None, 'tensor'), may hold values from -0.125 to 0.125
- w_down: bfloat16 [8192, 2048], P('tensor'), may hold values from -0.5 to 0.5
Outputs:
- layer_out: bfloat16 [8192, 2048], P(('dp', 'tensor'))
- in_grad: float32 [8192, 2048], P(('dp', 'tensor'))
- attn_gain_grad: float32 [2048], P(('dp', 'tensor'))
- mlp_gain_grad: float32 [2048], P(('dp', 'tensor'))
- w_query_grad: float32 [2048, 2048], P('dp', 'tensor')
- w_key_grad: float32 [2048, 512], P(('dp', 'tensor'))
- w_value_grad: float32 [2048, 512], P(('dp', 'tensor'))
- w_out_grad: float32 [2048, 2048], P('tensor', 'dp')
- w_gate_grad: float32 [2048, 8192], P('dp', 'tensor')
- w_up_grad: float32 [2048, 8192], P('dp', 'tensor')
- w_down_grad: float32 [8192, 2048], P('tensor', 'dp')
Inputs may be any that keep to these rules, and one draw needn't show every extreme that they name: `seq_lengths`: each sequence has between half of its 2048 slots and all of them valid; some sequence is full and some is exactly half full.
All inputs are finite; a program needn't handle non-finite values.
Results may differ from a plain program's by a relative error of at most 0.02.
Values may be sent and summed in bfloat16 or wider, within the bound.
No kernel may reach another device: no remote copies, remote signals or barrier semaphores. Data moves between devices by JAX's collectives and lax.ppermute only.
A program may use at most 256 MiB of HBM per device.

v0:
```python
import math
import jax
import jax.numpy as jnp
from jax import lax
from jax.sharding import PartitionSpec as P

H = 32
KVH = 8
HD = 64
SEQ_LEN = 2048
QB = 512
RESID = 0.22
ATTN_SCALE = 0.015625
EPSILON = 1e-05
THETA_LOG = math.log(10000000.0)
MASKED = -1e30


def rope_tables(count):
    positions = (jnp.arange(count, dtype=jnp.int32) % SEQ_LEN).astype(jnp.float32)[:, None]
    freqs = jnp.exp(-THETA_LOG * jnp.arange(0, HD, 2, dtype=jnp.int32).astype(jnp.float32) / HD)[
        None, :
    ]
    angle_rows = positions * freqs
    angle_rows = jnp.concatenate([angle_rows, angle_rows], 1)
    return (jnp.cos(angle_rows), jnp.sin(angle_rows))


def turn_half(values):
    half = HD // 2
    return jnp.concatenate([-values[..., half:], values[..., :half]], -1)


def rotate(values, cosines, sines):
    return values * cosines[:, None, :] + turn_half(values) * sines[:, None, :]


def unrotate(grads, cosines, sines):
    return grads * cosines[:, None, :] - turn_half(grads * sines[:, None, :])


def norm_rows(rows, gain):
    row_scale = lax.rsqrt(jnp.mean(rows * rows, axis=-1, keepdims=True) + EPSILON)
    return (rows * row_scale * gain, row_scale)


def norm_back(rows, row_scale, gain, incoming):
    normed = rows * row_scale
    scaled = incoming * gain
    return row_scale * (scaled - normed * jnp.mean(scaled * normed, axis=-1, keepdims=True))


def local(
    hidden_in,
    seq_lengths,
    out_grad,
    attn_gain,
    mlp_gain,
    w_query,
    w_key,
    w_value,
    w_out,
    w_gate,
    w_up,
    w_down,
):
    rows_total = hidden_in.shape[0]
    heads_here = w_query.shape[1] // HD
    groups = lax.axis_size("tensor")
    member = lax.axis_index("tensor")
    share = rows_total // groups
    share_start = member * share
    blocks = rows_total // QB
    bf16 = jnp.bfloat16
    f32 = jnp.float32
    over_rows = (((0,), (0,)), ((), ()))
    over_cols = (((1,), (1,)), ((), ()))
    cosines, sines = rope_tables(rows_total)
    inputs = hidden_in.astype(f32)
    normed_one, scale_one = norm_rows(inputs, attn_gain)
    normed_low = normed_one.astype(bf16)
    key_all, value_all = (
        lax.all_gather(w_key, "tensor", axis=0, tiled=True),
        lax.all_gather(w_value, "tensor", axis=0, tiled=True),
    )
    kv_head = member * heads_here // (H // KVH)
    key_cols = lax.dynamic_slice_in_dim(key_all, kv_head * HD, HD, 1)
    value_cols = lax.dynamic_slice_in_dim(value_all, kv_head * HD, HD, 1)
    query_raw = jnp.dot(normed_low, w_query, preferred_element_type=f32).reshape(
        rows_total, heads_here, HD
    )
    key_raw = jnp.dot(normed_low, key_cols, preferred_element_type=f32)
    value_raw = jnp.dot(normed_low, value_cols, preferred_element_type=f32)
    queries = rotate(query_raw, cosines, sines).astype(bf16)
    keys = rotate(key_raw[:, None, :], cosines, sines)[:, 0, :].astype(bf16)
    values = value_raw.astype(bf16)
    seq_slots = jnp.arange(seq_lengths.shape[0], dtype=jnp.int32)

    def block_inputs(index):
        start = index * QB
        seq_index = start // SEQ_LEN
        key_start = seq_index * SEQ_LEN
        length = jnp.sum(jnp.where(seq_slots == seq_index, seq_lengths, 0))
        query_rows = lax.dynamic_slice_in_dim(queries, start, QB, 0)
        raw = jnp.einsum("qhd,kd->hqk", query_rows, keys, preferred_element_type=f32) * ATTN_SCALE
        query_pos = start - key_start + jnp.arange(QB, dtype=jnp.int32)
        key_pos = jnp.arange(SEQ_LEN, dtype=jnp.int32)
        allowed = (key_pos[None, :] <= query_pos[:, None]) & (key_pos[None, :] < length)
        scores = jnp.where(allowed[None], raw, MASKED)
        return (start, key_start, query_rows, keys, values, scores)

    def forward_block(index):
        start, key_start, query_rows, key_rows, value_rows, scores = block_inputs(index)
        highest = jnp.max(scores, axis=-1, keepdims=True)
        expos = jnp.exp(scores - highest)
        totals = jnp.sum(expos, axis=-1, keepdims=True)
        probs = (expos / totals).astype(bf16)
        block_out = jnp.einsum("hqk,kd->qhd", probs, value_rows, preferred_element_type=f32)
        return (block_out, (highest + jnp.log(totals))[..., 0])

    attn_blocks, lse_blocks = lax.map(forward_block, jnp.arange(blocks, dtype=jnp.int32))
    attended = attn_blocks.reshape(rows_total, heads_here * HD).astype(bf16)
    attn_part = jnp.dot(attended, w_out, preferred_element_type=f32)
    attn_share = lax.psum_scatter(attn_part, "tensor", scatter_dimension=0, tiled=True)
    inputs_share = lax.dynamic_slice_in_dim(inputs, share_start, share, 0)
    scale_one_share = lax.dynamic_slice_in_dim(scale_one, share_start, share, 0)
    attn_full = lax.all_gather(attn_share, "tensor", axis=0, tiled=True)
    middle = inputs + RESID * attn_full
    normed_two, scale_two = norm_rows(middle, mlp_gain)
    normed_two_low = normed_two.astype(bf16)
    middle_share = lax.dynamic_slice_in_dim(middle, share_start, share, 0)
    scale_two_share = lax.dynamic_slice_in_dim(scale_two, share_start, share, 0)
    gate_rows = jnp.dot(normed_two_low, w_gate, preferred_element_type=f32)
    up_rows = jnp.dot(normed_two_low, w_up, preferred_element_type=f32)
    sigmoid_gate = jax.nn.sigmoid(gate_rows)
    silu_gate = gate_rows * sigmoid_gate
    activ = (silu_gate * up_rows).astype(bf16)
    mlp_part = jnp.dot(activ, w_down, preferred_element_type=f32)
    mlp_share = lax.psum_scatter(
        mlp_part.astype(jnp.bfloat16), "tensor", scatter_dimension=0, tiled=True
    ).astype(jnp.float32)
    layer_out = (middle_share + RESID * mlp_share).astype(bf16)
    row_ids = jnp.arange(rows_total, dtype=jnp.int32)
    length_rows = jnp.sum(
        jnp.where((row_ids // SEQ_LEN)[:, None] == seq_slots[None, :], seq_lengths[None, :], 0),
        axis=1,
    )
    valid_rows = (row_ids % SEQ_LEN < length_rows).astype(f32)[:, None]
    cotangent = out_grad.astype(f32) * valid_rows
    down_in = (RESID * cotangent).astype(bf16)
    down_wgrad = lax.dot_general(activ, down_in, over_rows, preferred_element_type=f32)
    activ_grad = lax.dot_general(down_in, w_down, over_cols, preferred_element_type=f32)
    gate_grad = (
        activ_grad * up_rows * sigmoid_gate * (1.0 + gate_rows * (1.0 - sigmoid_gate))
    ).astype(bf16)
    up_grad = (activ_grad * silu_gate).astype(bf16)
    gate_wgrad = lax.dot_general(normed_two_low, gate_grad, over_rows, preferred_element_type=f32)
    up_wgrad = lax.dot_general(normed_two_low, up_grad, over_rows, preferred_element_type=f32)
    norm_two_part = lax.dot_general(gate_grad, w_gate, over_cols, preferred_element_type=f32)
    norm_two_part = norm_two_part + lax.dot_general(
        up_grad, w_up, over_cols, preferred_element_type=f32
    )
    norm_two_share = lax.psum_scatter(norm_two_part, "tensor", scatter_dimension=0, tiled=True)
    norm_two_full = lax.all_gather(norm_two_share, "tensor", axis=0, tiled=True)
    middle_grad = cotangent + norm_back(middle, scale_two, mlp_gain, norm_two_full)
    branch_grad = (RESID * middle_grad).astype(bf16)
    middle_grad_share = lax.dynamic_slice_in_dim(middle_grad, share_start, share, 0)
    mlp_gain_part = jnp.sum(norm_two_share * middle_share * scale_two_share, axis=0)
    out_wgrad = lax.dot_general(attended, branch_grad, over_rows, preferred_element_type=f32)
    attended_grad = lax.dot_general(branch_grad, w_out, over_cols, preferred_element_type=f32)
    attended_grad = attended_grad.reshape(rows_total, heads_here, HD).astype(bf16)

    def backward_block(carry, index):
        key_grad, value_grad = carry
        start, key_start, query_rows, key_rows, value_rows, scores = block_inputs(index)
        lse_rows = lax.dynamic_index_in_dim(lse_blocks, index, 0, keepdims=False)
        probs = jnp.exp(scores - lse_rows[:, :, None])
        probs_low = probs.astype(bf16)
        grad_rows = lax.dynamic_slice_in_dim(attended_grad, start, QB, 0)
        value_part = jnp.einsum("hqk,qhd->khd", probs_low, grad_rows, preferred_element_type=f32)
        prob_grad = jnp.einsum("qhd,kd->hqk", grad_rows, value_rows, preferred_element_type=f32)
        row_delta = jnp.sum(prob_grad * probs, axis=-1, keepdims=True)
        score_grad = (probs * (prob_grad - row_delta)).astype(bf16)
        query_part = (
            jnp.einsum("hqk,kd->qhd", score_grad, key_rows, preferred_element_type=f32) * ATTN_SCALE
        )
        key_part = (
            jnp.einsum("hqk,qhd->khd", score_grad, query_rows, preferred_element_type=f32)
            * ATTN_SCALE
        )
        key_grad = key_grad + key_part
        value_grad = value_grad + value_part
        return ((key_grad, value_grad), query_part)

    empty_grad = jnp.zeros((rows_total, heads_here, HD), f32)
    (key_grad, value_grad), query_blocks = lax.scan(
        backward_block, (empty_grad, empty_grad), jnp.arange(blocks, dtype=jnp.int32)
    )
    query_grad = query_blocks.reshape(rows_total, heads_here, HD)
    query_low = (
        unrotate(query_grad, cosines, sines).reshape(rows_total, heads_here * HD).astype(bf16)
    )
    key_low = unrotate(key_grad, cosines, sines).reshape(rows_total, heads_here * HD).astype(bf16)
    value_low = value_grad.reshape(rows_total, heads_here * HD).astype(bf16)
    width = normed_low.shape[1]
    query_wgrad = lax.dot_general(normed_low, query_low, over_rows, preferred_element_type=f32)
    key_head_grad = (
        lax.dot_general(normed_low, key_low, over_rows, preferred_element_type=f32)
        .reshape(width, heads_here, HD)
        .sum(axis=1)
    )
    value_head_grad = (
        lax.dot_general(normed_low, value_low, over_rows, preferred_element_type=f32)
        .reshape(width, heads_here, HD)
        .sum(axis=1)
    )
    key_tiled = jnp.tile(key_cols, (1, heads_here))
    value_tiled = jnp.tile(value_cols, (1, heads_here))
    norm_one_part = lax.dot_general(query_low, w_query, over_cols, preferred_element_type=f32)
    norm_one_part = norm_one_part + lax.dot_general(
        key_low, key_tiled, over_cols, preferred_element_type=f32
    )
    norm_one_part = norm_one_part + lax.dot_general(
        value_low, value_tiled, over_cols, preferred_element_type=f32
    )
    norm_one_share = lax.psum_scatter(
        norm_one_part.astype(jnp.bfloat16), "tensor", scatter_dimension=0, tiled=True
    ).astype(jnp.float32)
    in_grad = middle_grad_share + norm_back(
        inputs_share, scale_one_share, attn_gain, norm_one_share
    )
    attn_gain_part = jnp.sum(norm_one_share * inputs_share * scale_one_share, axis=0)
    key_full = lax.dynamic_update_slice_in_dim(
        jnp.zeros(key_all.shape, f32), key_head_grad, kv_head * HD, 1
    )
    value_full = lax.dynamic_update_slice_in_dim(
        jnp.zeros(value_all.shape, f32), value_head_grad, kv_head * HD, 1
    )
    dense = (
        lax.psum_scatter(
            query_wgrad.astype(jnp.bfloat16), "dp", scatter_dimension=0, tiled=True
        ).astype(jnp.float32),
        lax.psum_scatter(
            gate_wgrad.astype(jnp.bfloat16), "dp", scatter_dimension=0, tiled=True
        ).astype(jnp.float32),
        lax.psum_scatter(
            up_wgrad.astype(jnp.bfloat16), "dp", scatter_dimension=0, tiled=True
        ).astype(jnp.float32),
        lax.psum_scatter(
            out_wgrad.astype(jnp.bfloat16), "dp", scatter_dimension=1, tiled=True
        ).astype(jnp.float32),
        lax.psum_scatter(
            down_wgrad.astype(jnp.bfloat16), "dp", scatter_dimension=1, tiled=True
        ).astype(jnp.float32),
    )
    shared = (
        lax.psum_scatter(key_full, ("dp", "tensor"), scatter_dimension=0, tiled=True),
        lax.psum_scatter(value_full, ("dp", "tensor"), scatter_dimension=0, tiled=True),
        lax.psum_scatter(attn_gain_part, ("dp", "tensor"), scatter_dimension=0, tiled=True),
        lax.psum_scatter(mlp_gain_part, ("dp", "tensor"), scatter_dimension=0, tiled=True),
    )
    return (
        layer_out,
        in_grad,
        shared[2],
        shared[3],
        dense[0],
        shared[0],
        shared[1],
        dense[3],
        dense[1],
        dense[2],
        dense[4],
    )


def solution(mesh):
    placed = (
        P("dp", None),
        P("dp"),
        P("dp", None),
        P(),
        P(),
        P(None, "tensor"),
        P("tensor", None),
        P("tensor", None),
        P("tensor", None),
        P(None, "tensor"),
        P(None, "tensor"),
        P("tensor", None),
    )
    return jax.shard_map(
        local,
        mesh=mesh,
        in_specs=placed,
        out_specs=(
            P(("dp", "tensor"), None),
            P(("dp", "tensor"), None),
            P(("dp", "tensor")),
            P(("dp", "tensor")),
            P("dp", "tensor"),
            P(("dp", "tensor"), None),
            P(("dp", "tensor"), None),
            P("tensor", "dp"),
            P("dp", "tensor"),
            P("dp", "tensor"),
            P("tensor", "dp"),
        ),
        check_vma=False,
    )
```

profile of v0, /device:TPU:0, one launch (start us, length us, event | category | flops | bytes accessed | tf_op | source)
XLA Modules:
  0.0 2185.7 jit_solution(15121321370525812363)
XLA Ops:
  14.7 8.7 multiply_convert_fusion.3
  23.5 5.8 fusion.99
  30.8 31.4 %all-gather.7.cloned.1.call-done = bf16[2048,512]{1,0:T(8,128)(2,1)} async-done(((bf16[256,512]{1,0:T(8,128)(2,1)}), bf16[2048,512]{1,0:T(8,128)(2,1)}) %all-gather.7.cloned.1.call-update) | async-done | bytes 2097168 | tf_op jit(solution)/shard_map/all_gather | solution.py:84
  62.2 49.9 %all-gather.5.cloned.1.call-done = bf16[2048,512]{1,0:T(8,128)(2,1)} async-done(((bf16[256,512]{1,0:T(8,128)(2,1)}), bf16[2048,512]{1,0:T(8,128)(2,1)}) %all-gather.5.cloned.1.call-update) | async-done | bytes 2097168 | tf_op jit(solution)/shard_map/all_gather | solution.py:83
  113.7 6.4 fusion.100
  120.2 6.2 convolution_convert_fusion.5
  130.9 70.8 %while.31 = (s32[]{:T(128)}, bf16[4,512,4,64]{1,3,2,0:T(8,128)(2,1)}, f32[4,4,512]{2,1,0:T(4,128)}, s32[4]{0:T(128)S(1)}, s32[1]{0:T(128)}, /*index=5*/bf16[2048...) while((s32[]{:T(128)}, ...), condition=%wide.region_4.5_spmd, body=%wide.region_1.4_spmd.sunk | while | flops 1126171136 | bytes 64299484 | solution.py:121
  160.1 5.2 fusion.160
  195.5 5.2 fusion.160
  205.2 8.2 fusion.101
  213.4 281.4 %reduce-scatter.12.cloned.1.call-done = f32[256,2048]{1,0:T(8,128)} async-done(((f32[2048,2048]{1,0:T(8,128)}), f32[256,2048]{1,0:T(8,128)}) %reduce-scatter.12.cloned.1.call-update) | async-done | bytes 2097168 | tf_op jit(solution)/shard_map/reduce_scatter | solution.py:124
  495.6 228.1 %all-gather.9.cloned.1.call-done = f32[2048,2048]{1,0:T(8,128)} async-done(((f32[256,2048]{1,0:T(8,128)}), f32[2048,2048]{1,0:T(8,128)}) %all-gather.9.cloned.1.call-update) | async-done | bytes 16777232 | tf_op jit(solution)/shard_map/all_gather | solution.py:127
  723.7 10.1 multiply_reduce_fusion.1
  733.9 5.8 copy-done.1
  741.9 11.0 fusion.102
  752.9 11.0 fusion.103
  763.9 23.4 %multiply_convert_fusion.4 = (bf16[2048,1024]{1,0:T(8,128)(2,1)}, bf16[2048,1024]{1,0:T(8,128)(2,1)}, bf16[2048,1024]{1,0:T(8,128)(2,1)}) fusion(f32[2048,1024]{1,0:T(8,128)} %fusion.102, f32[2048,1024]{1,0:T(8,128)} %fusion.103, bf16[1024,2048]{1,0:T(8,128)(2,1)} %param.27, bf16[2048,2048]{1,0:T(8,128)(2,1)} %param.18, f32[2048]{0:T(1024)S(1)} %fusion.94), kind=kOutput, calls=%fused_computation.75 | convolution fusion | flops 8638169088 | bytes 41951232 | tf_op jit(solution)/shard_map/dot_general | solution.py:152
  787.3 15.3 fusion.104
  802.6 17.2 convolution_add_fusion
  819.9 281.0 %reduce-scatter.16.cloned.1.call-done = f32[256,2048]{1,0:T(8,128)} async-done(((f32[2048,2048]{1,0:T(8,128)}), f32[256,2048]{1,0:T(8,128)}) %reduce-scatter.16.cloned.1.call-update) | async-done | bytes 2097168 | tf_op jit(solution)/shard_map/reduce_scatter | solution.py:163
  1100.9 14.1 convolution_convert_fusion.3
  1115.1 14.2 convolution_convert_fusion.2
  1129.4 14.7 convolution_convert_fusion.1
  1146.1 14.4 convolution_convert_fusion
  1160.6 169.0 %all-gather.11.cloned.1.call-done = f32[2048,2048]{1,0:T(8,128)} async-done(((f32[256,2048]{1,0:T(8,128)}), f32[2048,2048]{1,0:T(8,128)}) %all-gather.11.cloned.1.call-update) | async-done | bytes 16777232 | tf_op jit(solution)/shard_map/all_gather | solution.py:164
  1329.5 13.7 multiply_reduce_fusion
  1343.2 15.7 multiply_add_fusion
  1365.0 302.1 %while.32 = (s32[]{:T(128)}, f32[2048,4,64]{0,2,1:T(8,128)}, f32[2048,4,64]{0,2,1:T(8,128)}, f32[4,512,4,64]{1,0,3,2:T(4,128)}, s32[4]{0:T(128)S(1)}, /*index=5*...) while((s32[]{:T(128)}, f32[2048,4,64]{0,2,1:T(8,128)}, ...), condition=%wide.region_12.13_spmd.clone, body=%wide.region_10.12_spmd.clone.sunk | while | flops 2752119296 | bytes 239403760 | solution.py:196
  1366.4 9.2 fusion.169
  1380.7 16.7 fusion.171
  1399.9 11.1 fusion.172
  1411.0 6.5 fusion.173
  1417.5 8.5 fusion.174
  1430.4 11.2 dynamic_update_slice.36
  1442.9 9.3 fusion.169
  1457.3 15.2 fusion.171
  1474.4 11.3 fusion.172
  1485.7 7.2 fusion.173
  1492.9 8.5 fusion.174
  1505.8 11.2 dynamic_update_slice.36
  1518.2 9.3 fusion.169
  1532.5 15.3 fusion.171
  1549.8 11.1 fusion.172
  1560.8 7.4 fusion.173
  1568.2 8.5 fusion.174
  1581.1 11.1 dynamic_update_slice.36
  1593.5 9.2 fusion.169
  1607.7 15.2 fusion.171
  1624.8 11.0 fusion.172
  1635.8 7.1 fusion.173
  1642.9 8.5 fusion.174
  1655.8 11.1 dynamic_update_slice.36
  1687.3 10.8 fusion.80
  1702.0 9.5 fusion.84
  1711.5 16.1 fusion.46
  1728.8 5.8 fusion.68
  1737.5 5.9 dynamic_update_slice.26
  1743.7 7.1 fusion.71
  1753.6 5.9 dynamic_update_slice.27
  1759.5 11.3 convert_element_type.153
  1788.2 99.2 %reduce-scatter.18.cloned.1.call-done = bf16[256,2048]{1,0:T(8,128)(2,1)} async-done(((bf16[2048,2048]{1,0:T(8,128)(2,1)}), bf16[256,2048]{1,0:T(8,128)(2,1)}) %reduce-scatter.18.cloned.1.call-update) | async-done | bytes 1048592 | tf_op jit(solution)/shard_map/reduce_scatter | solution.py:226
  1890.1 41.4 %all-reduce.2 = (f32[2048]{0:T(1024)S(1)}, f32[2048]{0:T(1024)S(1)}) all-reduce(f32[2048]{0:T(1024)S(1)} %get-tuple-element.295, f32[2048]{0:T(1024)S(1)} %get-tuple-element.343), channel_id=6, replica_groups=mesh['dp'=4,'tensor'=8] {'dp','tensor'}, use_global_device_ids=true, to_apply=%region_16.17.clone | all-reduce | flops 4096 | bytes 32768
  1937.1 96.4 %reduce-scatter.22.cloned.1.call-done = f32[64,512]{1,0:T(8,128)} async-done(((f32[2048,512]{1,0:T(8,128)}), f32[64,512]{1,0:T(8,128)}) %reduce-scatter.22.cloned.1.call-update) | async-done | bytes 131088 | tf_op jit(solution)/shard_map/reduce_scatter | solution.py:257
  2033.5 145.4 %reduce-scatter.24.cloned.1.call-done = f32[64,512]{1,0:T(8,128)} async-done(((f32[2048,512]{1,0:T(8,128)}), f32[64,512]{1,0:T(8,128)}) %reduce-scatter.24.cloned.1.call-update) | async-done | bytes 131088 | tf_op jit(solution)/shard_map/reduce_scatter | solution.py:258
  (328 shorter events, 178.2 us)
Async XLA Ops:
  7.2 198.0 %copy-start = (bf16[256,2048]{1,0:T(8,128)(2,1)S(1)}, bf16[256,2048]{1,0:T(8,128)(2,1)}, u32[]{:S(2)}) copy-start(bf16[256,2048]{1,0:T(8,128)(2,1)} %param.24) | copy-start | bytes 3145732
  7.2 7.5 copy-start.31
  7.2 55.0 %all-gather.7.cloned.1.call-start = ((), (), s32[]{:S(2)}) async-start(), calls=%async_computation.12 | async-start | bytes 2359296 | tf_op jit(solution)/shard_map/all_gather | solution.py:84
  7.9 104.2 %all-gather.5.cloned.1.call-start = ((), (), s32[]{:S(2)}) async-start(), calls=%async_computation.11 | async-start | bytes 2359296 | tf_op jit(solution)/shard_map/all_gather | solution.py:83
  8.7 486.1 %reduce-scatter.12.cloned.1.call-start = ((), (), s32[]{:S(2)}) async-start(), calls=%async_computation.13 | async-start | bytes 18874368 | tf_op jit(solution)/shard_map/reduce_scatter | solution.py:124
  13.9 9.6 copy-start.35
  14.7 8.8 copy-start.21
  113.7 12.7 copy-start.15
  120.2 9.2 copy-start.9
  201.7 11.6 copy-start.5
  213.3 510.3 %all-gather.9.cloned.1.call-start = ((), (), s32[]{:S(2)}) async-start(), calls=%async_computation.14 | async-start | bytes 18874368 | tf_op jit(solution)/shard_map/all_gather | solution.py:127
  494.8 606.0 %reduce-scatter.16.cloned.1.call-start = ((), (), s32[]{:S(2)}) async-start(), calls=%async_computation.16 | async-start | bytes 18874368 | tf_op jit(solution)/shard_map/reduce_scatter | solution.py:163
  495.5 244.1 %copy-start.33 = (f32[2048]{0:T(1024)S(1)}, f32[2048]{0:T(1024)}, u32[]{:S(2)}) copy-start(f32[2048]{0:T(1024)} %param.20) | copy-start | bytes 24580
  741.9 11.0 copy-start.11
  741.9 11.0 copy-start.37
  787.3 15.3 copy-start.38
  819.8 509.7 %all-gather.11.cloned.1.call-start = ((), (), s32[]{:S(2)}) async-start(), calls=%async_computation.17 | async-start | bytes 18874368 | tf_op jit(solution)/shard_map/all_gather | solution.py:164
  1100.9 671.7 %reduce-scatter.28.cloned.1.call-start = ((), (), s32[]{:S(2)}) async-start(), calls=%async_computation.23 | async-start | bytes 5242880 | tf_op jit(solution)/shard_map/reduce_scatter | solution.py:243
  1115.1 660.3 %reduce-scatter.30.cloned.1.call-start = ((), (), s32[]{:S(2)}) async-start(), calls=%async_computation.24 | async-start | bytes 5242880 | tf_op jit(solution)/shard_map/reduce_scatter | solution.py:246
  1129.4 648.9 %reduce-scatter.32.cloned.1.call-start = ((), (), s32[]{:S(2)}) async-start(), calls=%async_computation.25 | async-start | bytes 5242880 | tf_op jit(solution)/shard_map/reduce_scatter | solution.py:252
  1129.4 14.8 copy-start.16
  1129.4 15.7 copy-start.18
  1144.2 637.0 %reduce-scatter.14.cloned.1.call-start = ((), (), s32[]{:S(2)}) async-start(), calls=%async_computation.15 | async-start | bytes 9437184 | tf_op jit(solution)/shard_map/reduce_scatter | solution.py:139
  1160.5 169.0 %copy-start.30 = (f32[2048]{0:T(1024)S(1)}, f32[2048]{0:T(1024)}, u32[]{:S(2)}) copy-start(f32[2048]{0:T(1024)} %copy-done.29) | copy-start | bytes 24580
  1160.5 169.0 %copy-start.34 = (f32[2048]{0:T(1024)S(1)}, f32[2048]{0:T(1024)}, u32[]{:S(2)}) copy-start(f32[2048]{0:T(1024)} %param.20) | copy-start | bytes 24580
  1160.5 624.1 %reduce-scatter.20.cloned.1.call-start = ((), (), s32[]{:S(2)}) async-start(), calls=%async_computation.19 | async-start | bytes 1310720 | tf_op jit(solution)/shard_map/reduce_scatter | solution.py:240
  1380.7 16.7 slice-start
  1380.7 16.7 slice-start.1
  1380.7 18.1 slice-start.2
  1380.7 19.2 slice-start.3
  1411.0 15.1 slice-start.4
  1417.5 8.6 slice-start.5
  1457.3 15.2 slice-start
  1457.3 15.2 slice-start.1
  1457.3 15.9 slice-start.2
  1457.3 17.1 slice-start.3
  1485.7 15.8 slice-start.4
  1492.9 8.6 slice-start.5
  1532.5 15.4 slice-start
  1532.5 15.4 slice-start.1
  1532.5 16.0 slice-start.2
  1532.5 17.2 slice-start.3
  1560.8 7.4 copy-start.39
  1560.8 15.9 slice-start.4
  1568.2 8.5 slice-start.5
  1607.7 15.3 slice-start
  1607.7 15.3 slice-start.1
  1607.7 15.9 slice-start.2
  1607.7 17.1 slice-start.3
  1635.8 15.6 slice-start.4
  1642.9 8.5 slice-start.5
  1683.9 102.5 %reduce-scatter.26.cloned.1.call-start = ((), (), s32[]{:S(2)}) async-start(), calls=%async_computation.22 | async-start | bytes 1310720 | tf_op jit(solution)/shard_map/reduce_scatter | solution.py:249
  1683.9 14.1 slice-start.6
  1687.2 10.8 slice-start.7
  1687.2 10.8 slice-start.8
  1687.2 10.8 slice-start.9
  1687.2 10.8 copy-start.7
  1701.5 10.0 copy-start.20
  1701.5 10.0 copy-start.22
  1701.5 185.9 %reduce-scatter.18.cloned.1.call-start = ((), (), s32[]{:S(2)}) async-start(), calls=%async_computation.18 | async-start | bytes 9437184 | tf_op jit(solution)/shard_map/reduce_scatter | solution.py:226
  1727.6 306.0 %reduce-scatter.22.cloned.1.call-start = ((), (), s32[]{:S(2)}) async-start(), calls=%async_computation.20 | async-start | bytes 4325376 | tf_op jit(solution)/shard_map/reduce_scatter | solution.py:257
  1743.4 435.5 %reduce-scatter.24.cloned.1.call-start = ((), (), s32[]{:S(2)}) async-start(), calls=%async_computation.21 | async-start | bytes 4325376 | tf_op jit(solution)/shard_map/reduce_scatter | solution.py:258
  1770.9 10.3 copy-start.10
  1772.5 114.8 %copy-start.32 = (f32[2048]{0:T(1024)S(1)}, f32[2048]{0:T(1024)}, u32[]{:S(2)}) copy-start(f32[2048]{0:T(1024)} %param.19) | copy-start | bytes 24580
  (37 other events, 153.7 us)
Sparse Core Ops, SparseCore 0:
  10.2 51.9 all-gather.6
  64.3 47.7 all-gather.4
  213.5 281.2 reduce-scatter.11
  497.0 226.6 all-gather.8
  819.9 280.8 reduce-scatter.15
  1102.8 226.6 all-gather.10
  1332.1 42.6 reduce-scatter.27
  1377.5 44.5 reduce-scatter.29
  1424.5 44.4 reduce-scatter.31
  1473.0 149.0 reduce-scatter.13
  1684.0 23.2 reduce-scatter.19
  1709.8 24.8 reduce-scatter.25
  1738.3 149.0 reduce-scatter.17
  1890.2 143.2 reduce-scatter.21
  2036.3 142.5 reduce-scatter.23
where the time goes:
time: 2200 us; the launch traced here: 2190 us
  waiting for transfers between devices  1380 us (63%)
  matrix products  437 us (20%)
  other arithmetic  178 us (8%)
  local copies, waits for them, and re-layouts  110 us (5%)
  blocking collectives  41.4 us (2%)
    reduce_scatter x1, waiting for transfers between devices, local(): lax.psum_scatter(attn_part, 'tensor', scatter_dimension=0, tiled=True)  281 us
    reduce_scatter x1, waiting for transfers between devices, local(): lax.psum_scatter(norm_two_part, 'tensor', scatter_dimension=0, tiled=True)  281 us
    all_gather x1, waiting for transfers between devices, local(): attn_full = lax.all_gather(attn_share, 'tensor', axis=0, tiled=True)  228 us
    all_gather x1, waiting for transfers between devices, local(): norm_two_full = lax.all_gather(norm_two_share, 'tensor', axis=0, tiled=True)  169 us
    reduce_scatter x1, waiting for transfers between devices, local(): lax.psum_scatter(value_full, ('dp', 'tensor'), scatter_dimension=0, tiled...  145 us
    reduce_scatter x1, waiting for transfers between devices, local(): lax.psum_scatter(norm_one_part.astype(jnp.bfloat16), 'tensor', scatter_di...  99.2 us
    reduce_scatter x1, waiting for transfers between devices, local(): lax.psum_scatter(key_full, ('dp', 'tensor'), scatter_dimension=0, tiled=T...  96.4 us
    dot_general x4, matrix products, backward_block(): jnp.einsum('qhd,kd->hqk', grad_rows, value_rows, preferred_element_type=f32)  62.5 us
  transfers between devices with their start and end apart: 15, of which 9 were waited for; matrix products, arithmetic and copies ran while one was open for 24% of the time, Pallas kernels for 0%

commit v1 on v0

--- a/solution.py
+++ b/solution.py
@@ -14,6 +14,18 @@
 EPSILON = 1e-05
 THETA_LOG = math.log(10000000.0)
 MASKED = -1e30
+
+
+def doubled_up(x, axis, dim):
+    ways, here, step = (lax.axis_size(axis), lax.axis_index(axis), x.shape[dim])
+    line, have = (x, 1)
+    while have < ways:
+        line = jnp.concatenate(
+            [line, lax.ppermute(line, axis, [(d, (d - have) % ways) for d in range(ways)])],
+            axis=dim,
+        )
+        have = 2 * have
+    return jnp.roll(line, here * step, axis=dim)
 
 
 def rope_tables(count):
@@ -80,7 +92,7 @@
     normed_one, scale_one = norm_rows(inputs, attn_gain)
     normed_low = normed_one.astype(bf16)
     key_all, value_all = (
-        lax.all_gather(w_key, "tensor", axis=0, tiled=True),
+        doubled_up(w_key, "tensor", 0),
         lax.all_gather(w_value, "tensor", axis=0, tiled=True),
     )
     kv_head = member * heads_here // (H // KVH)

time: 2200 us -> 2200 us (level)
    ppermute x0 -> x3, waiting for transfers between devices: none -> 71.4 us  [doubled_up(): lax.ppermute(line, axis, [(d, (d - have) % ways) for d in range(ways)])]
    all_gather x1 -> x0, waiting for transfers between devices: 49.9 us -> none  [local(): lax.all_gather(w_key, 'tensor', axis=0, tiled=True)]
    all_gather x1, waiting for transfers between devices: 31.4 us -> 0.01 us  [local(): lax.all_gather(w_value, 'tensor', axis=0, tiled=True)]
  transfers between devices with their start and end apart: 15 -> 17, of which waited for: 9 -> 9; matrix products, arithmetic and copies ran while one was open for 24% -> 24% of each run, Pallas kernels for 0% -> 0%
where the time goes in v1:
time: 2200 us; the launch traced here: 2190 us
  waiting for transfers between devices  1380 us (63%)
  matrix products  435 us (20%)
  other arithmetic  179 us (8%)
  local copies, waits for them, and re-layouts  114 us (5%)
  blocking collectives  41.1 us (2%)
    reduce_scatter x1, waiting for transfers between devices, local(): lax.psum_scatter(attn_part, 'tensor', scatter_dimension=0, tiled=True)  283 us
    reduce_scatter x1, waiting for transfers between devices, local(): lax.psum_scatter(norm_two_part, 'tensor', scatter_dimension=0, tiled=True)  281 us
    all_gather x1, waiting for transfers between devices, local(): attn_full = lax.all_gather(attn_share, 'tensor', axis=0, tiled=True)  228 us
    all_gather x1, waiting for transfers between devices, local(): norm_two_full = lax.all_gather(norm_two_share, 'tensor', axis=0, tiled=True)  169 us
    reduce_scatter x1, waiting for transfers between devices, local(): lax.psum_scatter(value_full, ('dp', 'tensor'), scatter_dimension=0, tiled...  145 us
    reduce_scatter x1, waiting for transfers between devices, local(): lax.psum_scatter(norm_one_part.astype(jnp.bfloat16), 'tensor', scatter_di...  102 us
    reduce_scatter x1, waiting for transfers between devices, local(): lax.psum_scatter(key_full, ('dp', 'tensor'), scatter_dimension=0, tiled=T...  96.9 us
    ppermute x3, waiting for transfers between devices, doubled_up(): lax.ppermute(line, axis, [(d, (d - have) % ways) for d in range(ways)])  71.4 us
  transfers between devices with their start and end apart: 17, of which 9 were waited for; matrix products, arithmetic and copies ran while one was open for 24% of the time, Pallas kernels for 0%

profile of v1, /device:TPU:0, one launch (start us, length us, event | category | flops | bytes accessed | tf_op | source)
XLA Modules:
  0.0 2188.0 jit_solution(13395437060146262256)
XLA Ops:
  7.2 6.1 collective-permute-start
  18.5 9.0 multiply_convert_fusion.3
  28.5 5.8 fusion.98
  34.3 10.8 collective-permute-done.1
  51.1 60.6 %collective-permute-done.2 = bf16[1024,512]{1,0:T(8,128)(2,1)} collective-permute-done((bf16[1024,512]{1,0:T(8,128)(2,1)}, bf16[1024,512]{1,0:T(8,128)(2,1)}, u32[]{:S(2)}, u32[]{:S(2)}) %collective-permute-start.2) | collective-permute-done | bytes 1048608 | tf_op jit(solution)/shard_map/ppermute | solution.py:24
  114.8 6.2 fusion.99
  128.6 6.0 convolution_convert_fusion.5
  134.7 69.5 %while.31 = (s32[]{:T(128)}, bf16[4,512,4,64]{1,3,2,0:T(8,128)(2,1)S(1)}, f32[4,4,512]{2,1,0:T(4,128)}, s32[4]{0:T(128)S(1)}, s32[1]{0:T(128)}, /*index=5*/bf16[...) while((s32[]{:T(128)}, ...), condition=%wide.region_4.5_spmd, body=%wide.region_1.4_spmd.sunk | while | flops 1126171136 | bytes 55910820 | solution.py:133
  146.2 5.2 fusion.160
  206.3 8.2 fusion.100
  214.6 282.5 %reduce-scatter.12.cloned.1.call-done = f32[256,2048]{1,0:T(8,128)} async-done(((f32[2048,2048]{1,0:T(8,128)}), f32[256,2048]{1,0:T(8,128)}) %reduce-scatter.12.cloned.1.call-update) | async-done | bytes 2097168 | tf_op jit(solution)/shard_map/reduce_scatter | solution.py:136
  497.8 228.3 %all-gather.6.cloned.1.call-done = f32[2048,2048]{1,0:T(8,128)} async-done(((f32[256,2048]{1,0:T(8,128)}), f32[2048,2048]{1,0:T(8,128)}) %all-gather.6.cloned.1.call-update) | async-done | bytes 16777232 | tf_op jit(solution)/shard_map/all_gather | solution.py:139
  726.1 10.0 multiply_reduce_fusion.1
  736.1 5.8 copy-done.1
  744.1 11.0 fusion.101
  755.1 11.0 fusion.102
  766.1 23.4 %multiply_convert_fusion.4 = (bf16[2048,1024]{1,0:T(8,128)(2,1)}, bf16[2048,1024]{1,0:T(8,128)(2,1)}, bf16[2048,1024]{1,0:T(8,128)(2,1)}) fusion(f32[2048,1024]{1,0:T(8,128)} %fusion.101, f32[2048,1024]{1,0:T(8,128)} %fusion.102, bf16[1024,2048]{1,0:T(8,128)(2,1)} %param.27, bf16[2048,2048]{1,0:T(8,128)(2,1)} %param.18, f32[2048]{0:T(1024)S(1)} %fusion.93), kind=kOutput, calls=%fused_computation.75 | convolution fusion | flops 8638169088 | bytes 41951232 | tf_op jit(solution)/shard_map/dot_general | solution.py:164
  789.5 15.3 fusion.103
  804.8 17.2 convolution_add_fusion
  822.1 281.0 %reduce-scatter.16.cloned.1.call-done = f32[256,2048]{1,0:T(8,128)} async-done(((f32[2048,2048]{1,0:T(8,128)}), f32[256,2048]{1,0:T(8,128)}) %reduce-scatter.16.cloned.1.call-update) | async-done | bytes 2097168 | tf_op jit(solution)/shard_map/reduce_scatter | solution.py:175
  1103.2 14.1 convolution_convert_fusion.3
  1117.4 14.2 convolution_convert_fusion.2
  1131.7 14.7 convolution_convert_fusion.1
  1148.3 14.4 convolution_convert_fusion
  1162.8 168.9 %all-gather.8.cloned.1.call-done = f32[2048,2048]{1,0:T(8,128)} async-done(((f32[256,2048]{1,0:T(8,128)}), f32[2048,2048]{1,0:T(8,128)}) %all-gather.8.cloned.1.call-update) | async-done | bytes 16777232 | tf_op jit(solution)/shard_map/all_gather | solution.py:176
  1331.7 13.7 multiply_reduce_fusion
  1345.5 15.7 multiply_add_fusion
  1367.2 302.2 %while.32 = (s32[]{:T(128)}, f32[2048,4,64]{0,2,1:T(8,128)}, f32[2048,4,64]{0,2,1:T(8,128)}, f32[4,512,4,64]{1,0,3,2:T(4,128)}, s32[4]{0:T(128)S(1)}, /*index=5*...) while((s32[]{:T(128)}, f32[2048,4,64]{0,2,1:T(8,128)}, ...), condition=%wide.region_12.13_spmd.clone, body=%wide.region_10.12_spmd.clone.sunk | while | flops 2752119296 | bytes 239403760 | solution.py:208
  1368.7 9.2 fusion.169
  1382.9 16.7 fusion.171
  1402.2 11.1 fusion.172
  1413.2 6.5 fusion.173
  1419.8 8.5 fusion.174
  1432.7 11.2 dynamic_update_slice.36
  1445.1 9.3 fusion.169
  1459.5 15.2 fusion.171
  1476.5 11.3 fusion.172
  1487.9 7.2 fusion.173
  1495.0 8.5 fusion.174
  1508.0 11.2 dynamic_update_slice.36
  1520.4 9.3 fusion.169
  1534.7 15.4 fusion.171
  1551.9 11.1 fusion.172
  1563.0 7.4 fusion.173
  1570.4 8.5 fusion.174
  1583.3 11.1 dynamic_update_slice.36
  1595.6 9.2 fusion.169
  1609.9 15.2 fusion.171
  1627.0 11.0 fusion.172
  1638.0 7.1 fusion.173
  1645.1 8.5 fusion.174
  1658.0 11.1 dynamic_update_slice.36
  1686.6 10.0 fusion.104
  1696.7 8.5 fusion.80
  1711.8 16.1 fusion.46
  1729.2 5.7 fusion.68
  1737.9 5.9 dynamic_update_slice.26
  1744.1 6.3 fusion.71
  1753.3 5.9 dynamic_update_slice.27
  1759.2 11.3 convert_element_type.153
  1788.0 102.3 %reduce-scatter.18.cloned.1.call-done = bf16[256,2048]{1,0:T(8,128)(2,1)} async-done(((bf16[2048,2048]{1,0:T(8,128)(2,1)}), bf16[256,2048]{1,0:T(8,128)(2,1)}) %reduce-scatter.18.cloned.1.call-update) | async-done | bytes 1048592 | tf_op jit(solution)/shard_map/reduce_scatter | solution.py:238
  1893.0 41.1 %all-reduce.2 = (f32[2048]{0:T(1024)S(1)}, f32[2048]{0:T(1024)S(1)}) all-reduce(f32[2048]{0:T(1024)S(1)} %get-tuple-element.295, f32[2048]{0:T(1024)S(1)} %get-tuple-element.343), channel_id=6, replica_groups=mesh['dp'=4,'tensor'=8] {'dp','tensor'}, use_global_device_ids=true, to_apply=%region_16.17.clone | all-reduce | flops 4096 | bytes 32768
  1939.6 96.9 %reduce-scatter.22.cloned.1.call-done = f32[64,512]{1,0:T(8,128)} async-done(((f32[2048,512]{1,0:T(8,128)}), f32[64,512]{1,0:T(8,128)}) %reduce-scatter.22.cloned.1.call-update) | async-done | bytes 131088 | tf_op jit(solution)/shard_map/reduce_scatter | solution.py:269
  2036.5 144.7 %reduce-scatter.24.cloned.1.call-done = f32[64,512]{1,0:T(8,128)} async-done(((f32[2048,512]{1,0:T(8,128)}), f32[64,512]{1,0:T(8,128)}) %reduce-scatter.24.cloned.1.call-update) | async-done | bytes 131088 | tf_op jit(solution)/shard_map/reduce_scatter | solution.py:270
  (333 shorter events, 188.3 us)
Async XLA Ops:
  7.2 199.2 %copy-start = (bf16[256,2048]{1,0:T(8,128)(2,1)S(1)}, bf16[256,2048]{1,0:T(8,128)(2,1)}, u32[]{:S(2)}) copy-start(bf16[256,2048]{1,0:T(8,128)(2,1)} %param.24) | copy-start | bytes 3145732
  7.2 11.3 copy-start.32
  7.2 119.3 %all-gather.4.cloned.1.call-start = ((), (), s32[]{:S(2)}) async-start(), calls=%async_computation.11 | async-start | bytes 2359296 | tf_op jit(solution)/shard_map/all_gather | solution.py:96
  7.2 20.3 collective-permute-start
  13.3 483.8 %reduce-scatter.12.cloned.1.call-start = ((), (), s32[]{:S(2)}) async-start(), calls=%async_computation.12 | async-start | bytes 18874368 | tf_op jit(solution)/shard_map/reduce_scatter | solution.py:136
  18.5 9.1 copy-start.36
  18.5 9.1 copy-start.20
  18.5 10.0 copy-start.26
  28.3 16.8 collective-permute-start.1
  28.5 17.4 copy-start.22
  46.9 64.7 %collective-permute-start.2 = (bf16[1024,512]{1,0:T(8,128)(2,1)}, bf16[1024,512]{1,0:T(8,128)(2,1)}, u32[]{:S(2)}, u32[]{:S(2)}) collective-permute-start(bf16[1024,512]{1,0:T(8,128)(2,1)} %pad_maximum_fusion.1), channel_id=1, source_target_pairs={{0,4},{1,5},{2,6},{3,7},{4,0},{5,1},{6,2},{7,3},{8,12},{9,13},{10,... | collective-permute-start | bytes 3145736 | tf_op jit(solution)/shard_map/ppermute | solution.py:24
  48.7 64.2 %copy-start.23 = (bf16[256,512]{1,0:T(8,128)(2,1)S(1)}, bf16[256,512]{1,0:T(8,128)(2,1)}, u32[]{:S(2)}) copy-start(bf16[256,512]{1,0:T(8,128)(2,1)} %copy-done.21) | copy-start | bytes 786436
  48.7 64.3 %copy-start.16 = (bf16[512,512]{1,0:T(8,128)(2,1)S(1)}, bf16[512,512]{1,0:T(8,128)(2,1)}, u32[]{:S(2)}) copy-start(bf16[512,512]{1,0:T(8,128)(2,1)} %copy-done.15) | copy-start | bytes 1572868
  114.8 9.2 copy-start.17
  204.2 10.3 copy-start.5
  214.5 511.6 %all-gather.6.cloned.1.call-start = ((), (), s32[]{:S(2)}) async-start(), calls=%async_computation.13 | async-start | bytes 18874368 | tf_op jit(solution)/shard_map/all_gather | solution.py:139
  497.1 606.0 %reduce-scatter.16.cloned.1.call-start = ((), (), s32[]{:S(2)}) async-start(), calls=%async_computation.15 | async-start | bytes 18874368 | tf_op jit(solution)/shard_map/reduce_scatter | solution.py:175
  497.8 244.0 %copy-start.34 = (f32[2048]{0:T(1024)S(1)}, f32[2048]{0:T(1024)}, u32[]{:S(2)}) copy-start(f32[2048]{0:T(1024)} %param.20) | copy-start | bytes 24580
  744.1 11.0 copy-start.9
  744.1 11.0 copy-start.38
  789.5 15.3 copy-start.39
  822.0 509.7 %all-gather.8.cloned.1.call-start = ((), (), s32[]{:S(2)}) async-start(), calls=%async_computation.16 | async-start | bytes 18874368 | tf_op jit(solution)/shard_map/all_gather | solution.py:176
  1103.1 669.1 %reduce-scatter.28.cloned.1.call-start = ((), (), s32[]{:S(2)}) async-start(), calls=%async_computation.22 | async-start | bytes 5242880 | tf_op jit(solution)/shard_map/reduce_scatter | solution.py:255
  1117.3 657.7 %reduce-scatter.30.cloned.1.call-start = ((), (), s32[]{:S(2)}) async-start(), calls=%async_computation.23 | async-start | bytes 5242880 | tf_op jit(solution)/shard_map/reduce_scatter | solution.py:258
  1131.6 646.2 %reduce-scatter.32.cloned.1.call-start = ((), (), s32[]{:S(2)}) async-start(), calls=%async_computation.24 | async-start | bytes 5242880 | tf_op jit(solution)/shard_map/reduce_scatter | solution.py:264
  1131.6 14.8 copy-start.18
  1131.7 15.7 copy-start.14
  1146.4 634.4 %reduce-scatter.14.cloned.1.call-start = ((), (), s32[]{:S(2)}) async-start(), calls=%async_computation.14 | async-start | bytes 9437184 | tf_op jit(solution)/shard_map/reduce_scatter | solution.py:151
  1162.7 169.0 %copy-start.31 = (f32[2048]{0:T(1024)S(1)}, f32[2048]{0:T(1024)}, u32[]{:S(2)}) copy-start(f32[2048]{0:T(1024)} %copy-done.30) | copy-start | bytes 24580
  1162.7 169.0 %copy-start.35 = (f32[2048]{0:T(1024)S(1)}, f32[2048]{0:T(1024)}, u32[]{:S(2)}) copy-start(f32[2048]{0:T(1024)} %param.20) | copy-start | bytes 24580
  1162.7 621.6 %reduce-scatter.20.cloned.1.call-start = ((), (), s32[]{:S(2)}) async-start(), calls=%async_computation.18 | async-start | bytes 1310720 | tf_op jit(solution)/shard_map/reduce_scatter | solution.py:252
  1382.9 16.7 slice-start
  1382.9 16.7 slice-start.1
  1382.9 18.1 slice-start.2
  1382.9 19.3 slice-start.3
  1413.2 15.1 slice-start.4
  1419.8 8.6 slice-start.5
  1459.5 15.2 slice-start
  1459.5 15.2 slice-start.1
  1459.5 15.9 slice-start.2
  1459.5 17.1 slice-start.3
  1487.9 15.8 slice-start.4
  1495.0 8.6 slice-start.5
  1534.7 15.4 slice-start
  1534.7 15.4 slice-start.1
  1534.7 16.0 slice-start.2
  1534.7 17.2 slice-start.3
  1563.0 15.9 slice-start.4
  1609.9 15.3 slice-start
  1609.9 15.3 slice-start.1
  1609.9 15.9 slice-start.2
  1609.9 17.1 slice-start.3
  1638.0 15.6 slice-start.4
  1686.5 10.1 copy-start.29
  1686.5 99.6 %reduce-scatter.26.cloned.1.call-start = ((), (), s32[]{:S(2)}) async-start(), calls=%async_computation.21 | async-start | bytes 1310720 | tf_op jit(solution)/shard_map/reduce_scatter | solution.py:261
  1686.6 10.1 copy-start.42
  1686.6 18.6 slice-start.6
  1686.6 18.6 slice-start.7
  1696.6 8.5 slice-start.8
  1708.6 181.7 %reduce-scatter.18.cloned.1.call-start = ((), (), s32[]{:S(2)}) async-start(), calls=%async_computation.17 | async-start | bytes 9437184 | tf_op jit(solution)/shard_map/reduce_scatter | solution.py:238
  1728.0 308.6 %reduce-scatter.22.cloned.1.call-start = ((), (), s32[]{:S(2)}) async-start(), calls=%async_computation.19 | async-start | bytes 4325376 | tf_op jit(solution)/shard_map/reduce_scatter | solution.py:269
  1743.8 437.4 %reduce-scatter.24.cloned.1.call-start = ((), (), s32[]{:S(2)}) async-start(), calls=%async_computation.20 | async-start | bytes 4325376 | tf_op jit(solution)/shard_map/reduce_scatter | solution.py:270
  1770.5 10.2 copy-start.8
  1772.2 118.1 %copy-start.33 = (f32[2048]{0:T(1024)S(1)}, f32[2048]{0:T(1024)}, u32[]{:S(2)}) copy-start(f32[2048]{0:T(1024)} %param.19) | copy-start | bytes 24580
  (35 other events, 169.5 us)
Sparse Core Ops, SparseCore 0:
  13.5 84.6 all-gather.3
  214.7 282.3 reduce-scatter.11
  499.4 226.6 all-gather.5
  822.1 280.9 reduce-scatter.15
  1105.1 226.6 all-gather.7
  1334.1 42.6 reduce-scatter.27
  1379.5 44.5 reduce-scatter.29
  1426.6 44.4 reduce-scatter.31
  1475.2 148.9 reduce-scatter.13
  1686.6 23.4 reduce-scatter.19
  1712.8 24.8 reduce-scatter.25
  1741.2 149.0 reduce-scatter.17
  1893.2 143.2 reduce-scatter.21
  2039.3 141.8 reduce-scatter.23
